TPU v7x, 32 devices: a whole 2x2x4 slice. The times are simulated.
32 devices in a mesh: feat: 4 (over y, x), tok: 8 (over z, core).
Axes of the slice: x: 2, y: 2, z: 4, core: 2. Of those that a mesh axis runs over, the one named last changes fastest.
Arguments:
- tokens: bfloat16 [2048, 12288], P('tok', 'feat'), may hold values from -6 to 6
- gate_weight: bfloat16 [16, 5, 768, 768], P('feat', None, 'tok'), may hold values from -0.09375 to 0.09375
- up_weight: bfloat16 [16, 5, 768, 768], P('feat', None, 'tok'), may hold values from -0.09375 to 0.09375
- gate_scale: float32 [16, 5], P('feat'), may hold values from 0.35 to 2.8
- up_scale: float32 [16, 5], P('feat'), may hold values from 0.35 to 2.8
- partners: int32 [16, 5], replicated, may hold values from 0 to 15, as said below
- latent_in: bfloat16 [12288, 768], P('feat'), may hold values from -0.0546875 to 0.0546875
- latent_out: bfloat16 [768, 12288], P(None, 'feat'), may hold values from -0.21875 to 0.21875
Outputs:
- hidden: bfloat16 [2048, 12288], P('tok', 'feat')
- rank_term: bfloat16 [2048, 12288], P('tok', 'feat')
Inputs may be any that keep to these rules, and one draw needn't show every extreme that they name: `partners`: row i lists the blocks i, i xor 1, i xor 2, i xor 4 and i xor 8, each once, in some order.
All inputs are finite; a program needn't handle non-finite values.
Results may differ from a plain program's by a relative error of at most 0.015.
Values may be sent and summed in bfloat16 or wider, within the bound.
A program may use at most 128 MiB of HBM per device.

v0:
```python
import jax
import jax.numpy as jnp
from jax import lax
from jax.sharding import PartitionSpec as P


def swapped(value, axis, bit):
    mask = 2**bit
    pairs = [(source, source ^ mask) for source in range(lax.axis_size(axis))]
    return lax.ppermute(value, axis, pairs)


def project_slots(inputs, weight_block):
    return jnp.einsum("jktb,jkbc->tjkc", inputs, weight_block, preferred_element_type=jnp.float32)


def per_device(
    tokens, gate_weight, up_weight, gate_scale, up_scale, partners, latent_in, latent_out
):
    tok_rows = tokens.shape[0]
    blocks = gate_weight.shape[0]
    slot_count = gate_weight.shape[1]
    blk_width = gate_weight.shape[3]
    feat_count = lax.axis_size("feat")
    local_bits = blocks.bit_length() - 1
    feat_bits = feat_count.bit_length() - 1
    pieces = tokens.reshape(tok_rows, blocks, blk_width)
    remote = []
    for bit_pos in range(feat_bits):
        remote.append(swapped(pieces, "feat", bit_pos))
    first_block = lax.axis_index("feat") * blocks
    slot_ids = jnp.arange(slot_count, dtype=jnp.int32)
    per_block = []
    for own_block in range(blocks):
        global_id = first_block + own_block
        candidates = [pieces[:, own_block]]
        labels = [global_id]
        for bit_pos in range(local_bits + feat_bits):
            if bit_pos < local_bits:
                candidates.append(pieces[:, own_block ^ 1 << bit_pos])
            else:
                candidates.append(remote[bit_pos - local_bits][:, own_block])
            labels.append(jnp.bitwise_xor(global_id, 1 << bit_pos))
        stacked = jnp.stack(candidates)
        wanted = lax.dynamic_index_in_dim(partners, global_id, 0, keepdims=False)
        matched = wanted[:, None] == jnp.stack(labels)[None, :]
        slot_order = jnp.sum(jnp.where(matched, slot_ids[None, :], 0), axis=1)
        per_block.append(jnp.take(stacked, slot_order, axis=0))
    inputs = jnp.stack(per_block)
    full_gate, full_up = (
        lax.all_gather(gate_weight, "tok", axis=2, tiled=True),
        lax.all_gather(up_weight, "tok", axis=2, tiled=True),
    )
    gate_terms = project_slots(inputs, full_gate)
    up_terms = project_slots(inputs, full_up)
    gate_sum = jnp.sum(gate_terms * gate_scale[None, :, :, None], axis=2)
    up_sum = jnp.sum(up_terms * up_scale[None, :, :, None], axis=2)
    hidden = (
        (jax.nn.silu(gate_sum) * up_sum).astype(jnp.bfloat16).reshape(tok_rows, blocks * blk_width)
    )
    partial_value = jnp.dot(hidden, latent_in, preferred_element_type=jnp.float32)
    row_share = lax.psum_scatter(
        partial_value.astype(jnp.bfloat16), "feat", scatter_dimension=0, tiled=True
    )
    latent = lax.all_gather(row_share, "feat", axis=0, tiled=True)
    rank_term = jnp.dot(latent, latent_out, preferred_element_type=jnp.float32).astype(jnp.bfloat16)
    return (hidden, rank_term)


def solution(mesh):
    placed = (
        P("tok", "feat"),
        P("feat", None, "tok", None),
        P("feat", None, "tok", None),
        P("feat", None),
        P("feat", None),
        P(),
        P("feat", None),
        P(None, "feat"),
    )
    return jax.shard_map(
        per_device,
        mesh=mesh,
        in_specs=placed,
        out_specs=(P("tok", "feat"), P("tok", "feat")),
        check_vma=False,
    )
```

profile of v0, /device:TPU:0, one launch (start us, length us, event | category | flops | bytes accessed | tf_op | source)
XLA Modules:
  0.0 500.7 jit_solution(14187899263493273735)
XLA Ops:
  10.7 3.0 collective-permute-start
  13.8 1.5 collective-permute-start.1
  17.9 0.8 fusion.17
  19.5 0.8 bitcast_dynamic-update-slice_fusion
  20.3 1.2 fusion.20
  21.6 0.8 bitcast_dynamic-update-slice_fusion.1
  22.4 1.0 fusion.13
  23.4 0.8 bitcast_dynamic-update-slice_fusion.2
  24.2 24.1 %collective-permute-done = bf16[256,4,768]{2,0,1:T(8,128)(2,1)} collective-permute-done((bf16[256,4,768]{2,0,1:T(8,128)(2,1)S(1)}, bf16[256,4,768]{2,0,1:T(8,128)(2,1)}, u32[]{:S(2)}, u32[]{:S(2)}) %collective-permute-start) | collective-permute-done | bytes 1572896 | tf_op jit(solution)/shard_map/ppermute | solution.py:10
  48.3 2.6 fusion.11
  50.8 2.5 fusion.10
  53.4 3.6 gather_fusion.2
  57.0 3.7 gather_fusion.1
  60.6 2.2 gather_fusion
  62.9 3.6 gather_fusion.3
  66.5 3.2 select_bitcast_fusion.1
  69.7 1.5 select_bitcast_fusion.2
  71.3 1.6 select_bitcast_fusion.3
  73.5 1.5 select_bitcast_fusion
  75.0 144.3 %all-gather.3.cloned.1.call-done = bf16[4,5,768,768]{3,2,1,0:T(8,128)(2,1)} async-done(((bf16[4,5,96,768]{3,2,1,0:T(8,128)(2,1)}), bf16[4,5,768,768]{3,2,1,0:T(8,128)(2,1)}) %all-gather.3.cloned.1.call-update) | async-done | bytes 23592976 | tf_op jit(solution)/shard_map/all_gather | solution.py:51
  219.3 19.6 %multiply_reduce_fusion.1 = f32[4,256,768]{2,1,0:T(8,128)} fusion(bf16[4,5,768,768]{3,2,1,0:T(8,128)(2,1)} %all-gather.3.cloned.1.call-done, f32[4,5]{1,0:T(4,128)S(1)} %copy-done.10, bf16[1,5,256,768]{3,2,1,0:T(8,128)(2,1)} %select_bitcast_fusion, bf16[1,5,256,768]{3,2,1,0:T(8,128)(2,1)S(1)} %copy-done.3, ...), kind=kOutput, calls=%fused_computation.5 | convolution fusion | flops 6058672128 | bytes 34603088 | tf_op jit(solution)/shard_map/jktb,jkbc->tjkc/dot_general | solution.py:14
  238.9 2.4 copy.51
  241.3 184.8 %all-gather.5.cloned.1.call-done = bf16[4,5,768,768]{3,2,1,0:T(8,128)(2,1)} async-done(((bf16[4,5,96,768]{3,2,1,0:T(8,128)(2,1)}), bf16[4,5,768,768]{3,2,1,0:T(8,128)(2,1)}) %all-gather.5.cloned.1.call-update) | async-done | bytes 23592976 | tf_op jit(solution)/shard_map/all_gather | solution.py:52
  426.1 18.6 %multiply_reduce_fusion = f32[4,256,768]{2,1,0:T(8,128)} fusion(bf16[4,5,768,768]{3,2,1,0:T(8,128)(2,1)} %all-gather.5.cloned.1.call-done, f32[4,5]{1,0:T(4,128)S(1)} %copy-done.11, bf16[1,5,256,768]{3,2,1,0:T(8,128)(2,1)} %select_bitcast_fusion, bf16[1,5,256,768]{3,2,1,0:T(8,128)(2,1)} %select_bitcast_fusion.1, ...), kind=kOutput, calls=%fused_computation.4 | convolution fusion | flops 6058672128 | bytes 34603088 | tf_op jit(solution)/shard_map/jktb,jkbc->tjkc/dot_general | solution.py:14
  444.7 3.5 copy.52
  448.2 2.8 fusion
  451.0 1.1 copy-done.2
  452.2 4.5 convolution_convert_fusion.1
  456.7 2.6 copy.53
  459.3 20.5 %reduce-scatter.2.cloned.1.call-done = bf16[64,768]{1,0:T(8,128)(2,1)} async-done(((bf16[256,768]{1,0:T(8,128)(2,1)}), bf16[64,768]{1,0:T(8,128)(2,1)}) %reduce-scatter.2.cloned.1.call-update) | async-done | bytes 98320 | tf_op jit(solution)/shard_map/reduce_scatter | solution.py:62
  479.7 9.5 %all_gather.11 = bf16[256,768]{1,0:T(8,128)(2,1)S(1)} all-gather(bf16[64,768]{1,0:T(8,128)(2,1)} %reduce-scatter.2.cloned.1.call-done), channel_id=1, replica_groups=mesh['feat'=4,'tok'=8] {'feat'}, dimensions={0}, use_global_device_ids=true | all-gather | bytes 491520 | tf_op jit(solution)/shard_map/all_gather | solution.py:65
  489.2 4.9 convolution_convert_fusion
  (52 shorter events, 7.7 us)
Async XLA Ops:
  7.2 212.1 %all-gather.3.cloned.1.call-start = ((), (), s32[]{:S(2)}) async-start(), calls=%async_computation.1 | async-start | bytes 26542080 | tf_op jit(solution)/shard_map/all_gather | solution.py:51
  7.9 1.4 copy-start.4
  7.9 418.2 %all-gather.5.cloned.1.call-start = ((), (), s32[]{:S(2)}) async-start(), calls=%async_computation.2 | async-start | bytes 26542080 | tf_op jit(solution)/shard_map/all_gather | solution.py:52
  8.7 471.1 %reduce-scatter.2.cloned.1.call-start = ((), (), s32[]{:S(2)}) async-start(), calls=%async_computation.3 | async-start | bytes 491520 | tf_op jit(solution)/shard_map/reduce_scatter | solution.py:62
  10.0 5.6 %copy-start.5 = (s32[16,5]{0,1:T(8,128)S(1)}, s32[16,5]{0,1:T(8,128)}, u32[]{:S(2)}) copy-start(s32[16,5]{0,1:T(8,128)} %param.15) | copy-start | bytes 964
  10.7 37.5 %collective-permute-start = (bf16[256,4,768]{2,0,1:T(8,128)(2,1)S(1)}, bf16[256,4,768]{2,0,1:T(8,128)(2,1)}, u32[]{:S(2)}, u32[]{:S(2)}) collective-permute-start(bf16[256,4,768]{2,0,1:T(8,128)(2,1)S(1)} %copy.45), channel_id=1, source_target_pairs={{0,8},{8,0},{16,24},{24,16},{1,9},{9,1},{17,25},{25,17},{2,10},{10... | collective-permute-start | bytes 4718600 | tf_op jit(solution)/shard_map/ppermute | solution.py:10
  13.8 37.1 %collective-permute-start.1 = (bf16[256,4,768]{2,0,1:T(8,128)(2,1)S(1)}, bf16[256,4,768]{2,0,1:T(8,128)(2,1)}, u32[]{:S(2)}, u32[]{:S(2)}) collective-permute-start(bf16[256,4,768]{2,0,1:T(8,128)(2,1)S(1)} %copy.45), channel_id=1, source_target_pairs={{0,16},{8,24},{16,0},{24,8},{1,17},{9,25},{17,1},{25,9},{2,18},{10... | collective-permute-start | bytes 4718600 | tf_op jit(solution)/shard_map/ppermute | solution.py:10
  62.9 3.6 copy-start.7
  66.5 3.2 copy-start.1
  66.5 3.2 copy-start.9
  69.7 1.5 copy-start.8
  71.2 2.3 copy-start
  71.3 2.3 copy-start.6
  73.5 145.8 %copy-start.3 = (bf16[1,5,256,768]{3,2,1,0:T(8,128)(2,1)S(1)}, bf16[1,5,256,768]{3,2,1,0:T(8,128)(2,1)}, u32[]{:S(2)}) copy-start(bf16[1,5,256,768]{3,2,1,0:T(8,128)(2,1)} %select_bitcast_fusion.1) | copy-start | bytes 5898244
  73.5 145.8 %copy-start.10 = (f32[4,5]{1,0:T(4,128)S(1)}, f32[4,5]{1,0:T(4,128)}, u32[]{:S(2)}) copy-start(f32[4,5]{1,0:T(4,128)} %param.13) | copy-start | bytes 244
  238.9 187.2 %copy-start.11 = (f32[4,5]{1,0:T(4,128)S(1)}, f32[4,5]{1,0:T(4,128)}, u32[]{:S(2)}) copy-start(f32[4,5]{1,0:T(4,128)} %param.14) | copy-start | bytes 244
  451.0 1.1 copy-start.2
Sparse Core Ops, SparseCore 0:
  9.6 209.6 all-gather.2
  220.9 205.1 all-gather.4
  456.8 22.8 reduce-scatter.1
where the time goes:
time: 501 us
  waiting for transfers between devices  375 us (75%)
  matrix products  47.6 us (10%)
  local copies, waits for them, and re-layouts  37.6 us (8%)
  between operations  13.9 us (3%)
  other arithmetic  12.5 us (2%)
  blocking collectives  9.47 us (2%)
    all_gather x1, waiting for transfers between devices, per_device(): lax.all_gather(up_weight, 'tok', axis=2, tiled=True)  185 us
    all_gather x1, waiting for transfers between devices, per_device(): lax.all_gather(gate_weight, 'tok', axis=2, tiled=True)  144 us
    dot_general x2, matrix products, project_slots(): jnp.einsum('jktb,jkbc->tjkc', inputs, weight_block, preferred_element_typ...  38.2 us
    ppermute x2, waiting for transfers between devices, swapped(): return lax.ppermute(value, axis, pairs)  24.1 us
    reduce_scatter x1, waiting for transfers between devices, per_device(): lax.psum_scatter(partial_value.astype(jnp.bfloat16), 'feat', scatter_dime...  20.5 us
    unnamed x34, local copies, waits for them, and re-layouts  14.5 us
    gather x4, local copies, waits for them, and re-layouts, per_device(): per_block.append(jnp.take(stacked, slot_order, axis=0))  13.1 us
  transfers between devices with their start and end apart: 5, of which 4 were waited for; matrix products, arithmetic and copies ran while one was open for 12% of the time, Pallas kernels for 0%

commit v1 on v0

v1 whole, which is shorter than its diff:
```python
import jax
import jax.numpy as jnp
from jax import lax
from jax.sharding import PartitionSpec as P


def swapped(value, axis, bit):
    mask = 2**bit
    pairs = [(source, source ^ mask) for source in range(lax.axis_size(axis))]
    return lax.ppermute(value, axis, pairs)


def per_device(
    tokens, gate_weight, up_weight, gate_scale, up_scale, partners, latent_in, latent_out
):
    tok_rows = tokens.shape[0]
    blocks, slot_count, part_rows, blk_width = gate_weight.shape
    feat_count = lax.axis_size("feat")
    tok_count = lax.axis_size("tok")
    local_bits = blocks.bit_length() - 1
    feat_bits = feat_count.bit_length() - 1

    pieces = tokens.T.reshape(blocks, tok_count, part_rows, tok_rows).transpose(1, 0, 2, 3)
    own = lax.all_to_all(pieces, "tok", 0, 0, tiled=True)
    own = own.transpose(1, 2, 0, 3).reshape(blocks, part_rows, tok_count * tok_rows)
    remote = [swapped(own, "feat", bit_pos) for bit_pos in range(feat_bits)]

    first_block = lax.axis_index("feat") * blocks
    slot_ids = jnp.arange(slot_count, dtype=jnp.int32)
    latent_part = jnp.zeros((tok_rows, latent_in.shape[1]), jnp.float32)
    hidden = []
    for own_block in range(blocks):
        global_id = first_block + own_block
        candidates = [own[own_block]]
        labels = [global_id]
        for bit_pos in range(local_bits + feat_bits):
            if bit_pos < local_bits:
                candidates.append(own[own_block ^ 1 << bit_pos])
            else:
                candidates.append(remote[bit_pos - local_bits][own_block])
            labels.append(jnp.bitwise_xor(global_id, 1 << bit_pos))
        wanted = lax.dynamic_index_in_dim(partners, global_id, 0, keepdims=False)
        matched = wanted[:, None] == jnp.stack(labels)[None, :]
        slot_of = jnp.sum(jnp.where(matched, slot_ids[:, None], 0), axis=0)
        scaled = []
        for weight, scale in ((gate_weight, gate_scale), (up_weight, up_scale)):
            picked = jnp.take(weight[own_block], slot_of, axis=0)
            factor = jnp.take(scale[own_block], slot_of, axis=0)
            scaled.append((picked * factor[:, None, None]).astype(jnp.bfloat16))
        both = jnp.concatenate(scaled, axis=2).reshape(slot_count * part_rows, 2 * blk_width)
        inputs = jnp.concatenate(candidates, axis=0)
        partial = lax.dot_general(
            inputs, both, (((0,), (0,)), ((), ())), preferred_element_type=jnp.float32
        ).astype(jnp.bfloat16)
        sums = lax.psum_scatter(partial, "tok", scatter_dimension=0, tiled=True)
        sums = sums.astype(jnp.float32)
        block_hidden = (jax.nn.silu(sums[:, :blk_width]) * sums[:, blk_width:]).astype(jnp.bfloat16)
        hidden.append(block_hidden)
        rows = latent_in[own_block * blk_width : (own_block + 1) * blk_width]
        latent_part += jnp.dot(block_hidden, rows, preferred_element_type=jnp.float32)
    latent = latent_part
    for bit_pos in range(feat_bits):
        share = latent.astype(jnp.bfloat16)
        latent = share.astype(jnp.float32) + swapped(share, "feat", bit_pos).astype(jnp.float32)
    latent = latent.astype(jnp.bfloat16)
    rank_term = jnp.dot(latent, latent_out, preferred_element_type=jnp.float32).astype(jnp.bfloat16)
    return (jnp.concatenate(hidden, axis=1), rank_term)


def solution(mesh):
    placed = (
        P("tok", "feat"),
        P("feat", None, "tok", None),
        P("feat", None, "tok", None),
        P("feat", None),
        P("feat", None),
        P(),
        P("feat", None),
        P(None, "feat"),
    )
    return jax.shard_map(
        per_device,
        mesh=mesh,
        in_specs=placed,
        out_specs=(P("tok", "feat"), P("tok", "feat")),
        check_vma=False,
    )
```

time: 501 us -> 418 us (0.83)
  waiting for transfers between devices: 375 us -> 306 us
  matrix products: 47.6 us -> 31.3 us
  blocking collectives: 9.47 us -> 0 us
  starting transfers between devices: 4.67 us -> 13 us
    all_gather x2 -> x0, waiting for transfers between devices: 329 us -> none  [the longest x1 185 us: per_device(): lax.all_gather(up_weight, 'tok', axis=2, tiled=True)]
    reduce_scatter x1 -> x4, waiting for transfers between devices: 20.5 us -> 237 us  [per_device(): sums = lax.psum_scatter(partial, 'tok', scatter_dimension=0, tiled=True)]
    all_to_all x0 -> x1, waiting for transfers between devices: none -> 22.3 us  [per_device(): own = lax.all_to_all(pieces, 'tok', 0, 0, tiled=True)]
    ppermute x2 -> x4, waiting for transfers between devices: 24.1 us -> 46 us  [swapped(): return lax.ppermute(value, axis, pairs)]
    dot_general x3 -> x8, matrix products: 42.7 us -> 28.7 us  [the longest x4 21.4 us: per_device(): lax.dot_general(inputs, both, (((0,), (0,)), ((), ())), preferred_element...]
    all_gather x1 -> x0, blocking collectives: 9.47 us -> none  [per_device(): latent = lax.all_gather(row_share, 'feat', axis=0, tiled=True)]
    convert_element_type x1 -> x13, other arithmetic: 2.79 us -> 11.7 us  [the longest x4 5.38 us: per_device(): scaled.append((picked * factor[:, None, None]).astype(jnp.bfloat16))]
    another operation x4 -> x0, other arithmetic: 7.78 us -> none  [per_device(): inputs = jnp.stack(per_block)]
  transfers between devices with their start and end apart: 5 -> 9, of which waited for: 4 -> 9; matrix products, arithmetic and copies ran while one was open for 12% -> 13% of each run, Pallas kernels for 0% -> 0%
where the time goes in v1:
time: 418 us; the launch traced here: 416 us
  waiting for transfers between devices  306 us (73%)
  local copies, waits for them, and re-layouts  36.7 us (9%)
  matrix products  31.3 us (7%)
  other arithmetic  15 us (4%)
  between operations  14.3 us (3%)
  starting transfers between devices  13 us (3%)
    reduce_scatter x4, waiting for transfers between devices, per_device(): sums = lax.psum_scatter(partial, 'tok', scatter_dimension=0, tiled=True)  237 us
    ppermute x4, waiting for transfers between devices, swapped(): return lax.ppermute(value, axis, pairs)  46 us
    all_to_all x1, waiting for transfers between devices, per_device(): own = lax.all_to_all(pieces, 'tok', 0, 0, tiled=True)  22.3 us
    dot_general x4, matrix products, per_device(): lax.dot_general(inputs, both, (((0,), (0,)), ((), ())), preferred_element...  21.4 us
    unnamed x49, local copies, waits for them, and re-layouts  11.6 us
    gather x8, local copies, waits for them, and re-layouts, per_device(): picked = jnp.take(weight[own_block], slot_of, axis=0)  11.3 us
  transfers between devices with their start and end apart: 9, of which 9 were waited for; matrix products, arithmetic and copies ran while one was open for 13% of the time, Pallas kernels for 0%

profile of v1, /device:TPU:0, one launch (start us, length us, event | category | flops | bytes accessed | tf_op | source)
XLA Modules:
  0.0 415.6 jit_solution(879585706169449015)
XLA Ops:
  7.2 1.7 copy.23
  10.1 6.5 %all-to-all-start = ((bf16[8,4,96,256]{3,2,1,0:T(8,128)(2,1)}), bf16[8,4,96,256]{3,2,1,0:T(8,128)(2,1)S(1)}, u32[]{:S(2)}, u32[]{:S(2)}) async-start(bf16[8,4,96,256]{3,2,1,0:T(8,128)(2,1)} %copy.24), calls=%async_computation | async-start | bytes 3145728 | tf_op jit(solution)/shard_map/all_to_all | solution.py:24
  17.3 3.1 slice_bitcast_fusion.7
  20.4 1.5 gather_fusion
  21.9 3.2 slice_bitcast_fusion.6
  25.1 2.6 gather_fusion.2
  29.1 1.8 multiply_convert_fusion.7
  32.1 22.3 %all-to-all-done = bf16[8,4,96,256]{3,2,1,0:T(8,128)(2,1)S(1)} async-done(((bf16[8,4,96,256]{3,2,1,0:T(8,128)(2,1)}), bf16[8,4,96,256]{3,2,1,0:T(8,128)(2,1)S(1)}, u32[]{:S(2)}, u32[]{:S(2)}) %all-to-all-start) | async-done | bytes 1572896 | tf_op jit(solution)/shard_map/all_to_all | solution.py:24
  54.6 1.6 collective-permute-start
  56.2 1.5 collective-permute-start.1
  58.4 32.1 %collective-permute-done = bf16[4,96,2048]{2,1,0:T(8,128)(2,1)S(1)} collective-permute-done((bf16[4,96,2048]{2,1,0:T(8,128)(2,1)S(1)}, bf16[4,96,2048]{2,1,0:T(8,128)(2,1)S(1)}, u32[]{:S(2)}, u32[]{:S(2)}) %collective-permute-start) | collective-permute-done | bytes 1572896 | tf_op jit(solution)/shard_map/ppermute | solution.py:10
  95.1 5.4 %convolution_convert_fusion.3 = bf16[2048,1536]{1,0:T(8,128)(2,1)} fusion(bf16[480,2048]{1,0:T(8,128)(2,1)S(1)} %get-tuple-element.24, bf16[480,1536]{1,0:T(8,128)(2,1)S(1)} %bitcast.142), kind=kOutput, calls=%fused_computation.19 | convolution fusion | flops 3023044608 | bytes 9732096 | tf_op jit(solution)/shard_map/dot_general | solution.py:52
  103.1 1.5 gather_fusion.6
  105.9 1.6 multiply_convert_fusion.5
  109.1 5.4 %convolution_convert_fusion.2 = bf16[2048,1536]{1,0:T(8,128)(2,1)} fusion(bf16[480,2048]{1,0:T(8,128)(2,1)S(1)} %copy-done.12, bf16[480,1536]{1,0:T(8,128)(2,1)S(1)} %bitcast.144), kind=kOutput, calls=%fused_computation.18 | convolution fusion | flops 3023044608 | bytes 9732096 | tf_op jit(solution)/shard_map/dot_general | solution.py:52
  117.0 1.5 gather_fusion.10
  119.9 1.6 multiply_convert_fusion.3
  123.0 5.3 %convolution_convert_fusion.1 = bf16[2048,1536]{1,0:T(8,128)(2,1)} fusion(bf16[480,2048]{1,0:T(8,128)(2,1)S(1)} %copy-done.8, bf16[480,1536]{1,0:T(8,128)(2,1)S(1)} %bitcast.145), kind=kOutput, calls=%fused_computation.17 | convolution fusion | flops 3023044608 | bytes 9732096 | tf_op jit(solution)/shard_map/dot_general | solution.py:52
  133.1 5.4 %convolution_convert_fusion = bf16[2048,1536]{1,0:T(8,128)(2,1)} fusion(bf16[480,2048]{1,0:T(8,128)(2,1)S(1)} %copy-done.10, bf16[480,1536]{1,0:T(8,128)(2,1)S(1)} %bitcast.143), kind=kOutput, calls=%fused_computation.16 | convolution fusion | flops 3023044608 | bytes 9732096 | tf_op jit(solution)/shard_map/dot_general | solution.py:52
  138.5 30.4 %reduce-scatter.5.cloned.1.call-done = bf16[256,1536]{1,0:T(8,128)(2,1)} async-done(((bf16[2048,1536]{1,0:T(8,128)(2,1)}), bf16[256,1536]{1,0:T(8,128)(2,1)}) %reduce-scatter.5.cloned.1.call-update) | async-done | bytes 786448 | tf_op jit(solution)/shard_map/reduce_scatter | solution.py:55
  170.2 69.2 %reduce-scatter.7.cloned.1.call-done = bf16[256,1536]{1,0:T(8,128)(2,1)} async-done(((bf16[2048,1536]{1,0:T(8,128)(2,1)}), bf16[256,1536]{1,0:T(8,128)(2,1)}) %reduce-scatter.7.cloned.1.call-update) | async-done | bytes 786448 | tf_op jit(solution)/shard_map/reduce_scatter | solution.py:55
  240.8 69.2 %reduce-scatter.9.cloned.1.call-done = bf16[256,1536]{1,0:T(8,128)(2,1)} async-done(((bf16[2048,1536]{1,0:T(8,128)(2,1)}), bf16[256,1536]{1,0:T(8,128)(2,1)}) %reduce-scatter.9.cloned.1.call-update) | async-done | bytes 786448 | tf_op jit(solution)/shard_map/reduce_scatter | solution.py:55
  312.0 68.3 %reduce-scatter.11.cloned.1.call-done = bf16[256,1536]{1,0:T(8,128)(2,1)} async-done(((bf16[2048,1536]{1,0:T(8,128)(2,1)}), bf16[256,1536]{1,0:T(8,128)(2,1)}) %reduce-scatter.11.cloned.1.call-update) | async-done | bytes 786448 | tf_op jit(solution)/shard_map/reduce_scatter | solution.py:55
  381.9 1.9 fusion.4
  383.8 1.8 convolution_add_fusion.2
  385.6 1.8 convolution_add_fusion.1
  387.4 1.8 fusion
  389.2 1.5 collective-permute-start.2
  390.7 7.5 %collective-permute-done.2 = bf16[256,768]{1,0:T(8,128)(2,1)S(1)} collective-permute-done((bf16[256,768]{1,0:T(8,128)(2,1)S(1)}, bf16[256,768]{1,0:T(8,128)(2,1)S(1)}, u32[]{:S(2)}, u32[]{:S(2)}) %collective-permute-start.2) | collective-permute-done | bytes 393248 | tf_op jit(solution)/shard_map/ppermute | solution.py:10
  398.3 1.5 collective-permute-start.3
  401.2 5.3 %collective-permute-done.3 = bf16[256,768]{1,0:T(8,128)(2,1)S(1)} collective-permute-done((bf16[256,768]{1,0:T(8,128)(2,1)S(1)}, bf16[256,768]{1,0:T(8,128)(2,1)S(1)}, u32[]{:S(2)}, u32[]{:S(2)}) %collective-permute-start.3) | collective-permute-done | bytes 393248 | tf_op jit(solution)/shard_map/ppermute | solution.py:10
  406.5 2.6 convolution_convert_fusion.4
  (114 shorter events, 33.0 us)
Async XLA Ops:
  10.1 6.7 %copy-start.13 = (s32[16,5]{0,1:T(8,128)S(1)}, s32[16,5]{0,1:T(8,128)}, u32[]{:S(2)}) copy-start(s32[16,5]{0,1:T(8,128)} %param.17) | copy-start | bytes 964
  10.1 44.3 %all-to-all-start = ((bf16[8,4,96,256]{3,2,1,0:T(8,128)(2,1)}), bf16[8,4,96,256]{3,2,1,0:T(8,128)(2,1)S(1)}, u32[]{:S(2)}, u32[]{:S(2)}) async-start(bf16[8,4,96,256]{3,2,1,0:T(8,128)(2,1)} %copy.24), calls=%async_computation | async-start | bytes 3145728 | tf_op jit(solution)/shard_map/all_to_all | solution.py:24
  16.6 152.3 %reduce-scatter.5.cloned.1.call-start = ((), (), s32[]{:S(2)}) async-start(), calls=%async_computation.5 | async-start | bytes 7077888 | tf_op jit(solution)/shard_map/reduce_scatter | solution.py:55
  21.9 5.8 %copy-start.14 = (f32[4,5]{1,0:T(4,128)S(1)}, f32[4,5]{1,0:T(4,128)}, u32[]{:S(2)}) copy-start(f32[4,5]{1,0:T(4,128)} %param.15) | copy-start | bytes 244
  25.1 3.3 copy-start.15
  54.6 35.9 %collective-permute-start = (bf16[4,96,2048]{2,1,0:T(8,128)(2,1)S(1)}, bf16[4,96,2048]{2,1,0:T(8,128)(2,1)S(1)}, u32[]{:S(2)}, u32[]{:S(2)}) collective-permute-start(bf16[4,96,2048]{2,1,0:T(8,128)(2,1)S(1)} %bitcast.135), channel_id=1, source_target_pairs={{0,8},{8,0},{16,24},{24,16},{1,9},{9,1},{17,25},{25,17},{2,10},{10... | collective-permute-start | bytes 4718600 | tf_op jit(solution)/shard_map/ppermute | solution.py:10
  56.2 35.6 %collective-permute-start.1 = (bf16[4,96,2048]{2,1,0:T(8,128)(2,1)S(1)}, bf16[4,96,2048]{2,1,0:T(8,128)(2,1)S(1)}, u32[]{:S(2)}, u32[]{:S(2)}) collective-permute-start(bf16[4,96,2048]{2,1,0:T(8,128)(2,1)S(1)} %bitcast.136), channel_id=1, source_target_pairs={{0,16},{8,24},{16,0},{24,8},{1,17},{9,25},{17,1},{25,9},{2,18},{10... | collective-permute-start | bytes 4718600 | tf_op jit(solution)/shard_map/ppermute | solution.py:10
  90.7 4.4 %copy-start.6 = (bf16[5,96,1536]{2,1,0:T(8,128)(2,1)S(1)}, bf16[5,96,1536]{2,1,0:T(8,128)(2,1)}, u32[]{:S(2)}) copy-start(bf16[5,96,1536]{2,1,0:T(8,128)(2,1)} %pad_maximum_fusion.1) | copy-start | bytes 4423684
  91.9 1.3 copy-start.7
  93.2 1.3 copy-start.9
  93.2 1.9 copy-start.11
  100.5 1.1 copy-start.2
  100.5 2.6 copy-start.3
  100.5 138.9 %reduce-scatter.7.cloned.1.call-start = ((), (), s32[]{:S(2)}) async-start(), calls=%async_computation.6 | async-start | bytes 7077888 | tf_op jit(solution)/shard_map/reduce_scatter | solution.py:55
  103.1 2.8 copy-start.4
  107.5 1.5 copy-start.12
  114.4 1.1 copy-start
  114.4 2.6 copy-start.1
  114.5 195.5 %reduce-scatter.9.cloned.1.call-start = ((), (), s32[]{:S(2)}) async-start(), calls=%async_computation.7 | async-start | bytes 7077888 | tf_op jit(solution)/shard_map/reduce_scatter | solution.py:55
  117.0 2.8 copy-start.5
  121.4 1.6 copy-start.8
  128.4 252.0 %reduce-scatter.11.cloned.1.call-start = ((), (), s32[]{:S(2)}) async-start(), calls=%async_computation.8 | async-start | bytes 7077888 | tf_op jit(solution)/shard_map/reduce_scatter | solution.py:55
  131.6 1.5 copy-start.10
  381.9 24.6 %slice-start = ((s8[4718592]{0:T(1024)(128)(4,1)}), s8[4194304]{0:T(1024)(128)(4,1)S(1)}, s32[]{:S(2)}) async-start(s8[4718592]{0:T(1024)(128)(4,1)} %bitcast.146), calls=%async_computation.9 | async-start | bytes 8388608
  385.6 20.9 %slice-start.1 = ((s8[4718592]{0:T(1024)(128)(4,1)}), s8[524288]{0:T(1024)(128)(4,1)S(1)}, s32[]{:S(2)}) async-start(s8[4718592]{0:T(1024)(128)(4,1)} %bitcast.146), calls=%async_computation.10 | async-start | bytes 1048576
  389.2 9.0 %collective-permute-start.2 = (bf16[256,768]{1,0:T(8,128)(2,1)S(1)}, bf16[256,768]{1,0:T(8,128)(2,1)S(1)}, u32[]{:S(2)}, u32[]{:S(2)}) collective-permute-start(bf16[256,768]{1,0:T(8,128)(2,1)S(1)} %fusion), channel_id=1, source_target_pairs={{0,8},{8,0},{16,24},{24,16},{1,9},{9,1},{17,25},{25,17},{2,10},{10... | collective-permute-start | bytes 1179656 | tf_op jit(solution)/shard_map/ppermute | solution.py:10
  398.3 8.2 %collective-permute-start.3 = (bf16[256,768]{1,0:T(8,128)(2,1)S(1)}, bf16[256,768]{1,0:T(8,128)(2,1)S(1)}, u32[]{:S(2)}, u32[]{:S(2)}) collective-permute-start(bf16[256,768]{1,0:T(8,128)(2,1)S(1)} %add_convert_fusion.1), channel_id=1, source_target_pairs={{0,16},{8,24},{16,0},{24,8},{1,17},{9,25},{17,1},{25,9},{2,18},{10... | collective-permute-start | bytes 1179656 | tf_op jit(solution)/shard_map/ppermute | solution.py:10
Sparse Core Ops, SparseCore 0:
  100.6 68.2 reduce-scatter.4
  171.2 68.1 reduce-scatter.6
  241.8 68.1 reduce-scatter.8
  312.1 68.1 reduce-scatter.10
